TPU v7x, 32 devices: a whole 2x2x4 slice. The times are simulated.
32 devices in a mesh: bank: 2 (over x), tmpl: 16 (over z, y, core).
Axes of the slice: x: 2, y: 2, z: 4, core: 2. Of those that a mesh axis runs over, the one named last changes fastest.
Arguments:
- strain_fast: bfloat16 [9216], replicated, may hold values from -6 to 6
- strain_half: bfloat16 [8704], replicated, may hold values from -6 to 6
- strain_quarter: bfloat16 [8448], replicated, may hold values from -6 to 6
- strain_eighth: bfloat16 [8320], replicated, may hold values from -6 to 6
- basis_taps: bfloat16 [8, 512, 8192], P('bank', 'tmpl'), parts along dimension 0, may hold values from -0.0625 to 0.0625
- recon_coeffs: bfloat16 [8, 4096, 512], P('bank', 'tmpl'), parts along dimension 0, may hold values from -0.25 to 0.25
Outputs:
- snr_series: bfloat16 [8192, 1024], P(('bank', 'tmpl')), parts along dimension 0
- peak_snr: float32 [2048], P('bank'), parts along dimension 0
There are 2 independent parts, one for each index of `bank`. A program takes and returns all parts, laid end to end along the dimension named above; an argument that names none is the same for every part. Nothing has to cross between parts.
All inputs are finite; a program needn't handle non-finite values.
Results may differ from a plain program's by a relative error of at most 0.0049.
Values may be sent and summed in bfloat16 or wider, within the bound.
A program may use at most 128 MiB of HBM per device.

v0:
```python
import functools

import jax
import jax.numpy as jnp
from jax import lax
from jax.experimental import pallas as pl
from jax.experimental.pallas import tpu as pltpu
from jax.sharding import PartitionSpec as P

LANES = 128
BLOCK = 256
UNROLL = 9
PARTS = 3
ACROSS, MATE = range(2)


def shifted_rows(rows_ref, filled, tiles):
    width = tiles * LANES
    zero = jnp.zeros((8, LANES), jnp.float32)
    rows = jnp.concatenate(
        [jnp.broadcast_to(rows_ref[m : m + 1, :], (8, LANES)) if m < filled else zero for m in range(tiles)], axis=1
    )
    index = lax.broadcasted_iota(jnp.int32, (8, width), 0)
    for bit in range(3):
        moved = pltpu.roll(rows, width - (1 << bit), 1)
        rows = jnp.where((index >> bit) & 1 == 1, moved, rows)
    return rows


def doubled(values):
    rows = values.shape[0]
    lane = lax.broadcasted_iota(jnp.int32, (rows, LANES), 1)
    pieces = []
    for tile in range(values.shape[1] // LANES):
        source = values[:, tile * LANES : (tile + 1) * LANES]
        for half in range(2):
            index = lane // 2 + half * (LANES // 2)
            pieces.append(jnp.take_along_axis(source, index, axis=1, mode="promise_in_bounds"))
    return jnp.concatenate(pieces, axis=1)


def kernel(n, counts, *refs):
    sections = len(counts)
    x_hbm = refs[:sections]
    taps_hbm, coef_hbm, snr_ref, peak_ref = refs[sections : sections + 4]
    gathered = refs[sections + 4 : 2 * sections + 4]
    x_refs = refs[2 * sections + 4 : 3 * sections + 4]
    scratch = refs[3 * sections + 4 :]
    wide, shifted, taps_ref, coef_ref, total_ref, series, peaks, local_sem, send_sem, recv_sem, psend_sem, precv_sem = scratch
    rows, tap_count = taps_hbm.shape[1], taps_hbm.shape[2]
    lead = taps_ref.shape[2] - tap_count - tail_of(counts, tap_count)
    lines = n // 4
    me = lax.axis_index("tmpl")
    core = lax.rem(me, 2)
    side = lax.rem(me // 2, 2)
    spot = me // 4

    def device(at, y, c):
        return at * 4 + y * 2 + c

    across, mate = device(spot, 1 - side, core), device(spot, side, 1 - core)

    barrier = pltpu.get_barrier_semaphore()
    for step in range(1, n):
        pl.semaphore_signal(barrier, inc=1, device_id={"tmpl": lax.rem(me + step, n)}, device_id_type=pl.DeviceIdType.MESH)

    taps_in = [
        pltpu.make_async_copy(taps_hbm.at[s], taps_ref.at[s, :, pl.ds(lead, tap_count)], local_sem.at[s])
        for s in range(sections)
    ]
    coef_in = pltpu.make_async_copy(coef_hbm, coef_ref, local_sem.at[sections])
    x_in = [pltpu.make_async_copy(x_hbm[s], x_refs[s], local_sem.at[sections + 1 + s]) for s in range(sections)]
    for s in range(sections):
        x_in[s].start()
        taps_in[s].start()
    coef_in.start()
    for s in range(sections):
        taps_ref[s, :, :lead] = jnp.zeros((rows, lead), jnp.bfloat16)
        after = taps_ref.shape[2] - lead - tap_count
        taps_ref[s, :, lead + tap_count :] = jnp.zeros((rows, after), jnp.bfloat16)

    def convolve(s, serve):
        width = min(BLOCK, counts[s])
        groups = counts[s] // width
        filled = x_refs[s].shape[0]
        x_in[s].wait()
        wide[:filled, :] = x_refs[s][...].astype(jnp.float32)
        shifted[...] = shifted_rows(wide, filled, shifted.shape[1] // LANES)
        taps_in[s].wait()
        steps = -(-(groups - 1 + tap_count // BLOCK) // UNROLL)
        window = (2 * UNROLL + 2) * LANES

        def body(step, total):
            start = pl.multiple_of(step * (UNROLL * BLOCK), BLOCK)
            base = shifted[:, pl.ds(start, window)]
            grown = [base] + [pltpu.roll(base, window - 8 * g, 1) for g in range(1, LANES // 8)]
            frames = jnp.concatenate(grown, axis=0).astype(jnp.bfloat16)
            weights = jnp.concatenate([frames[:, at : at + width] for at in range(0, UNROLL * BLOCK, LANES)], axis=0)
            left = jnp.concatenate(
                [
                    taps_ref[s, :, pl.ds(pl.multiple_of(start + (lead - a * BLOCK), BLOCK), UNROLL * BLOCK)]
                    for a in range(groups)
                ],
                axis=0,
            )
            return total + jnp.dot(left, weights, preferred_element_type=jnp.float32)

        total = jnp.zeros((groups * rows, width), jnp.float32)
        cuts = [steps * part // PARTS for part in range(PARTS + 1)]
        for part in range(PARTS):
            total = lax.fori_loop(cuts[part], cuts[part + 1], body, total)
            if part < PARTS - 1:
                serve(PARTS * s + part)
        out = total.astype(jnp.bfloat16)
        for a in range(groups):
            gathered[s][me, :, a * width : (a + 1) * width] = out[a * rows : (a + 1) * rows]

    def remote(s, slot, way, to):
        return pltpu.make_async_remote_copy(
            src_ref=gathered[s].at[slot],
            dst_ref=gathered[s].at[slot],
            send_sem=send_sem.at[s, way, slot],
            recv_sem=recv_sem.at[s, slot],
            device_id={"tmpl": to},
            device_id_type=pl.DeviceIdType.MESH,
        )

    def arrive(s, slot):
        remote(s, slot, MATE, mate).wait_recv()

    def own(s, done=False):
        def go(way, to):
            copy = remote(s, me, way, to)
            copy.wait_send() if done else copy.start()

        def far(k):
            pl.when(spot + k < lines)(lambda: go(MATE + 2 * k - 1, device(spot + k, side, core)))
            pl.when(spot - k >= 0)(lambda: go(MATE + 2 * k, device(spot - k, side, core)))

        go(ACROSS, across)
        for k in range(1, lines):
            far(k)
        go(MATE, mate)

    def along(s, k, done=False):
        def handle(origin):
            slot = device(origin, side, core)

            def run():
                if not done:
                    arrive(s, slot)
                for way, to in ((ACROSS, across), (MATE, mate)):
                    copy = remote(s, slot, way, to)
                    copy.wait_send() if done else copy.start()

            return run

        pl.when(spot - k >= 0)(handle(spot - k))
        pl.when(spot + k < lines)(handle(spot + k))

    def beside(s, k, done=False):
        def handle(origin):
            slot = device(origin, 1 - side, core)

            def run():
                if done:
                    remote(s, slot, MATE, mate).wait_send()
                else:
                    arrive(s, slot)
                    remote(s, slot, MATE, mate).start()

            return run

        if k == 0:
            handle(spot)()
        else:
            pl.when(spot - k >= 0)(handle(spot - k))
            pl.when(spot + k < lines)(handle(spot + k))

    def step_of(s, k):
        if k == 0:
            own(s)
        elif k < lines:
            along(s, k)
        elif k < 2 * lines:
            beside(s, k - lines)
        else:
            for at in range(lines):
                for y in range(2):
                    arrive(s, device(at, y, 1 - core))

    def combine(s):
        basis = gathered[s][...].reshape(n * rows, counts[s])
        return jnp.dot(coef_ref[s], basis, preferred_element_type=jnp.float32)

    plan, rest = {}, []
    for s in range(sections):
        for k in range(1, lines):
            part = PARTS * (s + 1) - 1 + 2 + 2 * k
            plan.setdefault(part, []).append((s, k)) if part < PARTS * sections - 1 else rest.append((s, k))
        for k in range(lines):
            part = PARTS * (s + 1) - 1 + 5 + 2 * k
            entry = (s, lines + k)
            plan.setdefault(part, []).append(entry) if part < PARTS * sections - 1 else rest.append(entry)
    along_first = [e for e in rest if e[1] < lines]
    later = [e for e in rest if e[1] >= lines]

    def serve(part):
        for at, k in plan.get(part, []):
            step_of(at, k)

    running = {}
    for s in range(sections):
        convolve(s, serve)
        if s == 0:
            pl.semaphore_wait(barrier, n - 1)
        own(s)
        serve(PARTS * (s + 1) - 1)
    coef_in.wait()
    for s in range(sections):
        for at, k in along_first:
            if at == s:
                step_of(at, k)
        for at, k in later:
            if at == s - 1:
                step_of(at, k)
    step_of(0, 2 * lines)
    total_ref[...] = combine(0)
    for at, k in later:
        if at == sections - 1:
            step_of(at, k)
    for s in range(1, sections):
        step_of(s, 2 * lines)
        running[s] = combine(s)

    upper = running[sections - 1]
    for s in reversed(range(1, sections - 1)):
        upper = running[s] + doubled(upper)
    total = total_ref[...] + doubled(upper)
    peaks[me] = jnp.max(jnp.abs(total), axis=0, keepdims=True)

    def peak_copy(slot, to):
        return pltpu.make_async_remote_copy(
            src_ref=peaks.at[slot],
            dst_ref=peaks.at[slot],
            send_sem=psend_sem.at[to],
            recv_sem=precv_sem.at[slot],
            device_id={"tmpl": to},
            device_id_type=pl.DeviceIdType.MESH,
        )

    others = [lax.rem(me + step, n) for step in range(1, n)]
    for other in others:
        peak_copy(me, other).start()
    series[...] = total.astype(jnp.bfloat16)
    series_out = pltpu.make_async_copy(series, snr_ref, local_sem.at[3 * sections])
    series_out.start()
    for s in range(sections):
        own(s, True)
        for k in range(1, lines):
            along(s, k, True)
        for k in range(lines):
            beside(s, k, True)
    for other in others:
        peak_copy(other, other).wait_recv()
    for other in others:
        peak_copy(me, other).wait_send()
    peak_ref[...] = jnp.max(peaks[...], axis=0)
    series_out.wait()


def tail_of(counts, tap_count):
    groups = max(counts) // BLOCK
    steps = -(-(groups - 1 + tap_count // BLOCK) // UNROLL)
    return steps * UNROLL * BLOCK - tap_count


def fused(n, streams, basis_taps, recon_coeffs):
    sections, rows, tap_count = basis_taps.shape
    templates, bases = recon_coeffs.shape[1:]
    counts = tuple(stream.shape[0] - tap_count for stream in streams)
    tail = tail_of(counts, tap_count)
    width = tap_count + tail + 2 * LANES
    lead = (max(counts) // BLOCK - 1) * BLOCK
    tiles = [stream.reshape(-1, LANES) for stream in streams]
    snr, peak = pl.pallas_call(
        functools.partial(kernel, n, counts),
        out_shape=(
            jax.ShapeDtypeStruct((templates, counts[0]), jnp.bfloat16),
            jax.ShapeDtypeStruct((1, counts[0]), jnp.float32),
        ),
        in_specs=[pl.BlockSpec(memory_space=pltpu.HBM)] * (sections + 2),
        out_specs=(pl.BlockSpec(memory_space=pltpu.HBM), pl.BlockSpec(memory_space=pltpu.VMEM)),
        scratch_shapes=[pltpu.VMEM((n, rows, count), jnp.bfloat16) for count in counts]
        + [pltpu.VMEM(tile.shape, jnp.bfloat16) for tile in tiles]
        + [
            pltpu.VMEM((max(tile.shape[0] for tile in tiles), LANES), jnp.float32),
            pltpu.VMEM((8, width), jnp.float32),
            pltpu.VMEM((sections, rows, lead + tap_count + tail), jnp.bfloat16),
            pltpu.VMEM((sections, templates, bases), jnp.bfloat16),
            pltpu.VMEM((templates, counts[0]), jnp.float32),
            pltpu.VMEM((templates, counts[0]), jnp.bfloat16),
            pltpu.VMEM((n, 1, counts[0]), jnp.float32),
            pltpu.SemaphoreType.DMA((3 * sections + 1,)),
            pltpu.SemaphoreType.DMA((sections, n // 2, n)),
            pltpu.SemaphoreType.DMA((sections, n)),
            pltpu.SemaphoreType.DMA((n,)),
            pltpu.SemaphoreType.DMA((n,)),
        ],
        compiler_params=pltpu.CompilerParams(collective_id=0, has_side_effects=True, vmem_limit_bytes=63500000),
    )(*tiles, basis_taps, recon_coeffs)
    return snr, peak.reshape(counts[0])


def correlate(strain, bases_dev):
    tap_count = bases_dev.shape[1]
    sample_count = strain.shape[0] - tap_count
    stride = min(256, sample_count)
    extent = stride + tap_count

    def frame_block(number):
        segment = lax.dynamic_slice_in_dim(strain, number * stride, extent)
        repeated = jnp.tile(segment, stride + 1)[: stride * (extent + 1)]
        frames = repeated.reshape(stride, extent + 1)[:, :tap_count]
        product = lax.dot_general(bases_dev, frames, (((1,), (1,)), ((), ())), preferred_element_type=jnp.float32)
        return product.astype(jnp.bfloat16)

    pieces = lax.map(frame_block, jnp.arange(sample_count // stride, dtype=jnp.int32))
    return jnp.transpose(pieces, (1, 0, 2)).reshape(bases_dev.shape[0], sample_count)


def general(streams, basis_taps, recon_coeffs):
    counts = [stream.shape[0] - basis_taps.shape[2] for stream in streams]
    joined = jnp.concatenate([correlate(stream, taps) for stream, taps in zip(streams, basis_taps)], axis=1)
    basis = lax.all_gather(joined, "tmpl", axis=0, tiled=True)
    running, end = None, basis.shape[1]
    for section in reversed(range(len(counts))):
        columns = basis[:, end - counts[section] : end]
        end -= counts[section]
        summed = jnp.dot(recon_coeffs[section], columns, preferred_element_type=jnp.float32)
        running = summed if running is None else summed + jnp.repeat(running, 2, axis=1)
    return running.astype(jnp.bfloat16), lax.pmax(jnp.max(jnp.abs(running), axis=0), "tmpl")


def suits(n, streams, basis_taps, recon_coeffs):
    tap_count = basis_taps.shape[2]
    counts = [stream.shape[0] - tap_count for stream in streams]
    return (
        n % 4 == 0
        and basis_taps.shape[1] % 16 == 0
        and recon_coeffs.shape[1] % 16 == 0
        and tap_count % BLOCK == 0
        and counts[0] % BLOCK == 0
        and all(c % BLOCK == 0 or c == LANES for c in counts)
        and all(a == 2 * b for a, b in zip(counts, counts[1:]))
    )


def solution(mesh):
    n = mesh.shape["tmpl"]

    def per_device(strain_fast, strain_half, strain_quarter, strain_eighth, basis_taps, recon_coeffs):
        streams = (strain_fast, strain_half, strain_quarter, strain_eighth)
        if suits(n, streams, basis_taps, recon_coeffs):
            return fused(n, streams, basis_taps, recon_coeffs)
        return general(streams, basis_taps, recon_coeffs)

    in_specs = (P(), P(), P(), P(), P("bank", "tmpl", None), P("bank", "tmpl", None))
    out_specs = (P(("bank", "tmpl"), None), P("bank"))
    return jax.shard_map(per_device, mesh=mesh, in_specs=in_specs, out_specs=out_specs, check_vma=False)
```

profile of v0, /device:TPU:0, one launch (start us, length us, event | category | flops | bytes accessed | tf_op | source)
XLA Modules:
  0.0 40.5 jit_solution(17509745392094280288)
XLA Ops:
  0.6 36.8 %shard_map.77 = (bf16[256,1024]{1,0:T(8,128)(2,1)}, f32[1,1024]{1,0:T(1,128)}) custom-call(bf16[72,128]{1,0:T(8,128)(2,1)} %bitcast.5, bf16[68,128]{1,0:T(8,128)(2,1)} %bitcast.6, bf16[66,128]{1,0:T(8,128)(2,1)} %bitcast.7, bf16[65,128]{1,0:T(8,128)(2,1)} %bitcast.8, bf16[4,32,8192]{2,1,0:T(8,128)(2,1)} %refs_4_.1, bf16[4,256,512]{2,1,0:T(8,128)(2,1)} %refs_5_.1), custom_call_target="tpu_custom_call" | custom-call | tf_op jit(solution)/shard_map/pallas_call | solution.py:286
  37.4 1.9 %copy.10 = bf16[256,1024]{1,0:T(8,128)(2,1)} copy(bf16[256,1024]{1,0:T(8,128)(2,1)} %get-tuple-element.8) | data formatting | bytes 1048576
  39.3 1.3 %copy.11 = f32[1024]{0:T(1024)} copy(f32[1024]{0:T(1024)} %bitcast.9) | data formatting | bytes 8192
where the time goes:
time: 40.7 us; the launch traced here: 40.5 us
  Pallas kernels  36.8 us (90%)
  local copies, waits for them, and re-layouts  3.13 us (8%)
  between operations  0.64 us (2%)
    pallas_call x1, Pallas kernels, fused(): pl.pallas_call(functools.partial(kernel, n, counts), out_shape=(jax.Shape...  36.8 us
    unnamed x2, local copies, waits for them, and re-layouts  3.13 us

commit v1 on v0

--- a/solution.py
+++ b/solution.py
@@ -11,7 +11,6 @@
 BLOCK = 256
 UNROLL = 9
 PARTS = 3
-ACROSS, MATE = range(2)
 
 
 def shifted_rows(rows_ref, filled, tiles):
@@ -46,7 +45,8 @@
     gathered = refs[sections + 4 : 2 * sections + 4]
     x_refs = refs[2 * sections + 4 : 3 * sections + 4]
     scratch = refs[3 * sections + 4 :]
-    wide, shifted, taps_ref, coef_ref, total_ref, series, peaks, local_sem, send_sem, recv_sem, psend_sem, precv_sem = scratch
+    wide, shifted, taps_ref, coef_ref, total_ref, series, peaks = scratch[:7]
+    local_sem, along_sem, across_sem, mate_sem, recv_sem, pair_sem, peak_sem = scratch[7:]
     rows, tap_count = taps_hbm.shape[1], taps_hbm.shape[2]
     lead = taps_ref.shape[2] - tap_count - tail_of(counts, tap_count)
     lines = n // 4
@@ -79,7 +79,7 @@
         after = taps_ref.shape[2] - lead - tap_count
         taps_ref[s, :, lead + tap_count :] = jnp.zeros((rows, after), jnp.bfloat16)
 
-    def convolve(s, serve):
+    def convolve(s):
         width = min(BLOCK, counts[s])
         groups = counts[s] // width
         filled = x_refs[s].shape[0]
@@ -109,129 +109,94 @@
         cuts = [steps * part // PARTS for part in range(PARTS + 1)]
         for part in range(PARTS):
             total = lax.fori_loop(cuts[part], cuts[part + 1], body, total)
-            if part < PARTS - 1:
-                serve(PARTS * s + part)
         out = total.astype(jnp.bfloat16)
         for a in range(groups):
             gathered[s][me, :, a * width : (a + 1) * width] = out[a * rows : (a + 1) * rows]
 
-    def remote(s, slot, way, to):
+    def remote(s, part, send_sem, recv_sem, to):
         return pltpu.make_async_remote_copy(
-            src_ref=gathered[s].at[slot],
-            dst_ref=gathered[s].at[slot],
-            send_sem=send_sem.at[s, way, slot],
-            recv_sem=recv_sem.at[s, slot],
+            src_ref=gathered[s].at[part],
+            dst_ref=gathered[s].at[part],
+            send_sem=send_sem.at[s],
+            recv_sem=recv_sem,
             device_id={"tmpl": to},
             device_id_type=pl.DeviceIdType.MESH,
         )
 
-    def arrive(s, slot):
-        remote(s, slot, MATE, mate).wait_recv()
-
-    def own(s, done=False):
-        def go(way, to):
-            copy = remote(s, me, way, to)
-            copy.wait_send() if done else copy.start()
-
-        def far(k):
-            pl.when(spot + k < lines)(lambda: go(MATE + 2 * k - 1, device(spot + k, side, core)))
-            pl.when(spot - k >= 0)(lambda: go(MATE + 2 * k, device(spot - k, side, core)))
-
-        go(ACROSS, across)
-        for k in range(1, lines):
-            far(k)
-        go(MATE, mate)
-
-    def along(s, k, done=False):
-        def handle(origin):
+    def to_line(s, slot, to):
+        return remote(s, slot, along_sem, recv_sem.at[s, slot // 2], to)
+
+    def to_across(s, slot):
+        return remote(s, slot, across_sem, recv_sem.at[s, slot // 2], across)
+
+    def to_mate(s, part):
+        return remote(s, part, mate_sem, pair_sem.at[s], mate)
+
+    def both_ways(k, handle):
+        for way in (1, -1):
+            origin = spot - way * k
+            pl.when((origin >= 0) & (origin < lines))(functools.partial(handle, origin, spot + way))
+
+    def own(s):
+        to_across(s, me).start()
+        for way in (1, -1):
+            to = spot + way
+            pl.when((to >= 0) & (to < lines))(lambda to=to: to_line(s, me, device(to, side, core)).start())
+        to_mate(s, me).start()
+
+    def along(s, k):
+        def handle(origin, onward):
             slot = device(origin, side, core)
-
-            def run():
-                if not done:
-                    arrive(s, slot)
-                for way, to in ((ACROSS, across), (MATE, mate)):
-                    copy = remote(s, slot, way, to)
-                    copy.wait_send() if done else copy.start()
-
-            return run
-
-        pl.when(spot - k >= 0)(handle(spot - k))
-        pl.when(spot + k < lines)(handle(spot + k))
-
-    def beside(s, k, done=False):
-        def handle(origin):
+            to_across(s, slot).wait_recv()
+            pl.when((onward >= 0) & (onward < lines))(lambda: to_line(s, slot, device(onward, side, core)).start())
+            to_across(s, slot).start()
+            to_mate(s, slot).start()
+
+        both_ways(k, handle)
+
+    def beside(s, k):
+        def handle(origin, onward):
             slot = device(origin, 1 - side, core)
-
-            def run():
-                if done:
-                    remote(s, slot, MATE, mate).wait_send()
-                else:
-                    arrive(s, slot)
-                    remote(s, slot, MATE, mate).start()
-
-            return run
-
-        if k == 0:
-            handle(spot)()
-        else:
-            pl.when(spot - k >= 0)(handle(spot - k))
-            pl.when(spot + k < lines)(handle(spot + k))
-
-    def step_of(s, k):
-        if k == 0:
-            own(s)
-        elif k < lines:
-            along(s, k)
-        elif k < 2 * lines:
-            beside(s, k - lines)
-        else:
-            for at in range(lines):
-                for y in range(2):
-                    arrive(s, device(at, y, 1 - core))
+            to_across(s, slot).wait_recv()
+            to_mate(s, slot).start()
+
+        handle(spot, None) if k == 0 else both_ways(k, handle)
+
+    def some(count):
+        return pl.ds(0, count)
+
+    def sent(s):
+        to_mate(s, some(2 * lines)).wait_send()
+        remote(s, some(lines), across_sem, pair_sem.at[s], across).wait_send()
+        for at in range(lines):
+            count = (at + 1 if at < lines - 1 else 0) + (lines - at if at > 0 else 0)
+            if count:
+                pl.when(spot == at)(lambda count=count: remote(s, some(count), along_sem, pair_sem.at[s], mate).wait_send())
 
     def combine(s):
         basis = gathered[s][...].reshape(n * rows, counts[s])
         return jnp.dot(coef_ref[s], basis, preferred_element_type=jnp.float32)
 
-    plan, rest = {}, []
-    for s in range(sections):
-        for k in range(1, lines):
-            part = PARTS * (s + 1) - 1 + 2 + 2 * k
-            plan.setdefault(part, []).append((s, k)) if part < PARTS * sections - 1 else rest.append((s, k))
-        for k in range(lines):
-            part = PARTS * (s + 1) - 1 + 5 + 2 * k
-            entry = (s, lines + k)
-            plan.setdefault(part, []).append(entry) if part < PARTS * sections - 1 else rest.append(entry)
-    along_first = [e for e in rest if e[1] < lines]
-    later = [e for e in rest if e[1] >= lines]
-
-    def serve(part):
-        for at, k in plan.get(part, []):
-            step_of(at, k)
-
     running = {}
     for s in range(sections):
-        convolve(s, serve)
+        convolve(s)
         if s == 0:
             pl.semaphore_wait(barrier, n - 1)
         own(s)
-        serve(PARTS * (s + 1) - 1)
     coef_in.wait()
-    for s in range(sections):
-        for at, k in along_first:
-            if at == s:
-                step_of(at, k)
-        for at, k in later:
-            if at == s - 1:
-                step_of(at, k)
-    step_of(0, 2 * lines)
-    total_ref[...] = combine(0)
-    for at, k in later:
-        if at == sections - 1:
-            step_of(at, k)
-    for s in range(1, sections):
-        step_of(s, 2 * lines)
-        running[s] = combine(s)
+    for k in range(1, lines):
+        for s in range(sections):
+            along(s, k)
+        for s in range(sections):
+            beside(s, k - 1)
+    for s in range(sections):
+        beside(s, lines - 1)
+    for s in range(sections):
+        to_mate(s, some(2 * lines)).wait_recv()
+        if s == 0:
+            total_ref[...] = combine(0)
+        else:
+            running[s] = combine(s)
 
     upper = running[sections - 1]
     for s in reversed(range(1, sections - 1)):
@@ -239,12 +204,12 @@
     total = total_ref[...] + doubled(upper)
     peaks[me] = jnp.max(jnp.abs(total), axis=0, keepdims=True)
 
-    def peak_copy(slot, to):
+    def peak_copy(part, to):
         return pltpu.make_async_remote_copy(
-            src_ref=peaks.at[slot],
-            dst_ref=peaks.at[slot],
-            send_sem=psend_sem.at[to],
-            recv_sem=precv_sem.at[slot],
+            src_ref=peaks.at[part],
+            dst_ref=peaks.at[part],
+            send_sem=peak_sem.at[0],
+            recv_sem=peak_sem.at[1],
             device_id={"tmpl": to},
             device_id_type=pl.DeviceIdType.MESH,
         )
@@ -256,15 +221,9 @@
     series_out = pltpu.make_async_copy(series, snr_ref, local_sem.at[3 * sections])
     series_out.start()
     for s in range(sections):
-        own(s, True)
-        for k in range(1, lines):
-            along(s, k, True)
-        for k in range(lines):
-            beside(s, k, True)
-    for other in others:
-        peak_copy(other, other).wait_recv()
-    for other in others:
-        peak_copy(me, other).wait_send()
+        sent(s)
+    peak_copy(some(n - 1), mate).wait_recv()
+    peak_copy(some(n - 1), mate).wait_send()
     peak_ref[...] = jnp.max(peaks[...], axis=0)
     series_out.wait()
 
@@ -302,10 +261,12 @@
             pltpu.VMEM((templates, counts[0]), jnp.bfloat16),
             pltpu.VMEM((n, 1, counts[0]), jnp.float32),
             pltpu.SemaphoreType.DMA((3 * sections + 1,)),
-            pltpu.SemaphoreType.DMA((sections, n // 2, n)),
-            pltpu.SemaphoreType.DMA((sections, n)),
-            pltpu.SemaphoreType.DMA((n,)),
-            pltpu.SemaphoreType.DMA((n,)),
+            pltpu.SemaphoreType.DMA((sections,)),
+            pltpu.SemaphoreType.DMA((sections,)),
+            pltpu.SemaphoreType.DMA((sections,)),
+            pltpu.SemaphoreType.DMA((sections, n // 2)),
+            pltpu.SemaphoreType.DMA((sections,)),
+            pltpu.SemaphoreType.DMA((2,)),
         ],
         compiler_params=pltpu.CompilerParams(collective_id=0, has_side_effects=True, vmem_limit_bytes=63500000),
     )(*tiles, basis_taps, recon_coeffs)

time: 40.7 us -> 33.2 us (0.82)
  Pallas kernels: 36.8 us -> 29.2 us
    pallas_call x1, Pallas kernels: 36.8 us -> 29.2 us  [fused(): pl.pallas_call(functools.partial(kernel, n, counts), out_shape=(jax.Shape...]
where the time goes in v1:
time: 33.2 us; the launch traced here: 33 us
  Pallas kernels  29.2 us (88%)
  local copies, waits for them, and re-layouts  3.13 us (9%)
  between operations  0.64 us (2%)
    pallas_call x1, Pallas kernels, fused(): pl.pallas_call(functools.partial(kernel, n, counts), out_shape=(jax.Shape...  29.2 us
    unnamed x2, local copies, waits for them, and re-layouts  3.13 us

profile of v1, /device:TPU:0, one launch (start us, length us, event | category | flops | bytes accessed | tf_op | source)
XLA Modules:
  0.0 33.0 jit_solution(3997848845974384721)
XLA Ops:
  0.6 29.2 %shard_map.77 = (bf16[256,1024]{1,0:T(8,128)(2,1)}, f32[1,1024]{1,0:T(1,128)}) custom-call(bf16[72,128]{1,0:T(8,128)(2,1)} %bitcast.5, bf16[68,128]{1,0:T(8,128)(2,1)} %bitcast.6, bf16[66,128]{1,0:T(8,128)(2,1)} %bitcast.7, bf16[65,128]{1,0:T(8,128)(2,1)} %bitcast.8, bf16[4,32,8192]{2,1,0:T(8,128)(2,1)} %refs_4_.1, bf16[4,256,512]{2,1,0:T(8,128)(2,1)} %refs_5_.1), custom_call_target="tpu_custom_call" | custom-call | tf_op jit(solution)/shard_map/pallas_call | solution.py:245
  29.8 1.9 %copy.10 = bf16[256,1024]{1,0:T(8,128)(2,1)} copy(bf16[256,1024]{1,0:T(8,128)(2,1)} %get-tuple-element.8) | data formatting | bytes 1048576
  31.7 1.3 %copy.11 = f32[1024]{0:T(1024)} copy(f32[1024]{0:T(1024)} %bitcast.9) | data formatting | bytes 8192

commit v2 on v1

--- a/solution.py
+++ b/solution.py
@@ -45,8 +45,8 @@
     gathered = refs[sections + 4 : 2 * sections + 4]
     x_refs = refs[2 * sections + 4 : 3 * sections + 4]
     scratch = refs[3 * sections + 4 :]
-    wide, shifted, taps_ref, coef_ref, total_ref, series, peaks = scratch[:7]
-    local_sem, along_sem, across_sem, mate_sem, recv_sem, pair_sem, peak_sem = scratch[7:]
+    wide, shifted, taps_ref, coef_ref, total_ref, peaks = scratch[:6]
+    local_sem, along_sem, across_sem, mate_sem, recv_sem, pair_sem, peak_sem = scratch[6:]
     rows, tap_count = taps_hbm.shape[1], taps_hbm.shape[2]
     lead = taps_ref.shape[2] - tap_count - tail_of(counts, tap_count)
     lines = n // 4
@@ -61,8 +61,15 @@
     across, mate = device(spot, 1 - side, core), device(spot, side, 1 - core)
 
     barrier = pltpu.get_barrier_semaphore()
-    for step in range(1, n):
-        pl.semaphore_signal(barrier, inc=1, device_id={"tmpl": lax.rem(me + step, n)}, device_id_type=pl.DeviceIdType.MESH)
+
+    def greet(to):
+        pl.semaphore_signal(barrier, inc=1, device_id={"tmpl": to}, device_id_type=pl.DeviceIdType.MESH)
+
+    greet(mate)
+    greet(across)
+    pl.when(spot + 1 < lines)(lambda: greet(device(spot + 1, side, core)))
+    pl.when(spot - 1 >= 0)(lambda: greet(device(spot - 1, side, core)))
+    greeted = 2 + (spot + 1 < lines).astype(jnp.int32) + (spot - 1 >= 0).astype(jnp.int32)
 
     taps_in = [
         pltpu.make_async_copy(taps_hbm.at[s], taps_ref.at[s, :, pl.ds(lead, tap_count)], local_sem.at[s])
@@ -79,7 +86,7 @@
         after = taps_ref.shape[2] - lead - tap_count
         taps_ref[s, :, lead + tap_count :] = jnp.zeros((rows, after), jnp.bfloat16)
 
-    def convolve(s):
+    def convolve(s, serve):
         width = min(BLOCK, counts[s])
         groups = counts[s] // width
         filled = x_refs[s].shape[0]
@@ -109,94 +116,112 @@
         cuts = [steps * part // PARTS for part in range(PARTS + 1)]
         for part in range(PARTS):
             total = lax.fori_loop(cuts[part], cuts[part + 1], body, total)
+            if part < PARTS - 1:
+                serve((s, part))
         out = total.astype(jnp.bfloat16)
         for a in range(groups):
             gathered[s][me, :, a * width : (a + 1) * width] = out[a * rows : (a + 1) * rows]
 
-    def remote(s, part, send_sem, recv_sem, to):
+    chunks = chunks_of(counts, rows)
+
+    def remote(c, slot, send_sem, recv_sem, to):
+        s, first, height = chunks[c]
+        part = gathered[s].at[slot, pl.ds(first, height)]
         return pltpu.make_async_remote_copy(
-            src_ref=gathered[s].at[part],
-            dst_ref=gathered[s].at[part],
-            send_sem=send_sem.at[s],
+            src_ref=part,
+            dst_ref=part,
+            send_sem=send_sem.at[c],
             recv_sem=recv_sem,
             device_id={"tmpl": to},
             device_id_type=pl.DeviceIdType.MESH,
         )
 
-    def to_line(s, slot, to):
-        return remote(s, slot, along_sem, recv_sem.at[s, slot // 2], to)
-
-    def to_across(s, slot):
-        return remote(s, slot, across_sem, recv_sem.at[s, slot // 2], across)
-
-    def to_mate(s, part):
-        return remote(s, part, mate_sem, pair_sem.at[s], mate)
+    def to_line(c, slot, to):
+        return remote(c, slot, along_sem, recv_sem.at[c, slot // 2], to)
+
+    def to_across(c, slot):
+        return remote(c, slot, across_sem, recv_sem.at[c, slot // 2], across)
+
+    def to_mate(c, slot):
+        return remote(c, slot, mate_sem, pair_sem.at[c], mate)
 
     def both_ways(k, handle):
         for way in (1, -1):
             origin = spot - way * k
             pl.when((origin >= 0) & (origin < lines))(functools.partial(handle, origin, spot + way))
 
-    def own(s):
-        to_across(s, me).start()
+    def own(c):
+        to_across(c, me).start()
         for way in (1, -1):
             to = spot + way
-            pl.when((to >= 0) & (to < lines))(lambda to=to: to_line(s, me, device(to, side, core)).start())
-        to_mate(s, me).start()
-
-    def along(s, k):
+            pl.when((to >= 0) & (to < lines))(lambda to=to: to_line(c, me, device(to, side, core)).start())
+        to_mate(c, me).start()
+
+    def along(c, k):
         def handle(origin, onward):
             slot = device(origin, side, core)
-            to_across(s, slot).wait_recv()
-            pl.when((onward >= 0) & (onward < lines))(lambda: to_line(s, slot, device(onward, side, core)).start())
-            to_across(s, slot).start()
-            to_mate(s, slot).start()
+            to_across(c, slot).wait_recv()
+            to_across(c, slot).start()
+            pl.when((onward >= 0) & (onward < lines))(lambda: to_line(c, slot, device(onward, side, core)).start())
+            to_mate(c, slot).start()
 
         both_ways(k, handle)
 
-    def beside(s, k):
+    def beside(c, k):
         def handle(origin, onward):
             slot = device(origin, 1 - side, core)
-            to_across(s, slot).wait_recv()
-            to_mate(s, slot).start()
+            to_across(c, slot).wait_recv()
+            to_mate(c, slot).start()
 
         handle(spot, None) if k == 0 else both_ways(k, handle)
 
     def some(count):
         return pl.ds(0, count)
 
-    def sent(s):
-        to_mate(s, some(2 * lines)).wait_send()
-        remote(s, some(lines), across_sem, pair_sem.at[s], across).wait_send()
+    def sent(c):
+        to_mate(c, some(2 * lines)).wait_send()
+        remote(c, some(lines), across_sem, pair_sem.at[c], across).wait_send()
         for at in range(lines):
             count = (at + 1 if at < lines - 1 else 0) + (lines - at if at > 0 else 0)
             if count:
-                pl.when(spot == at)(lambda count=count: remote(s, some(count), along_sem, pair_sem.at[s], mate).wait_send())
+                pl.when(spot == at)(lambda count=count: remote(c, some(count), along_sem, pair_sem.at[c], mate).wait_send())
 
     def combine(s):
         basis = gathered[s][...].reshape(n * rows, counts[s])
         return jnp.dot(coef_ref[s], basis, preferred_element_type=jnp.float32)
 
+    pieces = range(len(chunks))
+    early = {}
+    order = []
+    for k in range(1, lines):
+        order += [(along, c, k) for c in pieces] + [(beside, c, k - 1) for c in pieces]
+    order += [(beside, c, lines - 1) for c in pieces]
+    done = set()
+
+    def serve(at):
+        for event in early.get(at, []):
+            event[0](*event[1:])
+            done.add(event)
+
     running = {}
     for s in range(sections):
-        convolve(s)
+        convolve(s, serve)
         if s == 0:
-            pl.semaphore_wait(barrier, n - 1)
-        own(s)
+            pl.semaphore_wait(barrier, greeted)
+        for c, chunk in enumerate(chunks):
+            if chunk[0] == s:
+                own(c)
+        serve((s, PARTS - 1))
     coef_in.wait()
-    for k in range(1, lines):
-        for s in range(sections):
-            along(s, k)
-        for s in range(sections):
-            beside(s, k - 1)
-    for s in range(sections):
-        beside(s, lines - 1)
-    for s in range(sections):
-        to_mate(s, some(2 * lines)).wait_recv()
-        if s == 0:
+    for event in order:
+        if event not in done:
+            event[0](*event[1:])
+    for c, chunk in enumerate(chunks):
+        to_mate(c, some(2 * lines)).wait_recv()
+        if chunk[0] == 0 and chunk[1] > 0 or chunk[2] == rows and chunk[0] == 0:
             total_ref[...] = combine(0)
-        else:
-            running[s] = combine(s)
+        elif chunk[0] > 0:
+            running[chunk[0]] = combine(chunk[0])
 
     upper = running[sections - 1]
     for s in reversed(range(1, sections - 1)):
@@ -217,15 +242,18 @@
     others = [lax.rem(me + step, n) for step in range(1, n)]
     for other in others:
         peak_copy(me, other).start()
-    series[...] = total.astype(jnp.bfloat16)
-    series_out = pltpu.make_async_copy(series, snr_ref, local_sem.at[3 * sections])
-    series_out.start()
-    for s in range(sections):
-        sent(s)
+    snr_ref[...] = total.astype(jnp.bfloat16)
+    for c in range(len(chunks)):
+        sent(c)
     peak_copy(some(n - 1), mate).wait_recv()
     peak_copy(some(n - 1), mate).wait_send()
     peak_ref[...] = jnp.max(peaks[...], axis=0)
-    series_out.wait()
+
+
+def chunks_of(counts, rows):
+    halves = 2 if rows % 32 == 0 else 1
+    height = rows // halves
+    return [(0, height * half, height) for half in range(halves)] + [(s, 0, rows) for s in range(1, len(counts))]
 
 
 def tail_of(counts, tap_count):
@@ -241,6 +269,7 @@
     tail = tail_of(counts, tap_count)
     width = tap_count + tail + 2 * LANES
     lead = (max(counts) // BLOCK - 1) * BLOCK
+    pieces = len(chunks_of(counts, rows))
     tiles = [stream.reshape(-1, LANES) for stream in streams]
     snr, peak = pl.pallas_call(
         functools.partial(kernel, n, counts),
@@ -249,7 +278,7 @@
             jax.ShapeDtypeStruct((1, counts[0]), jnp.float32),
         ),
         in_specs=[pl.BlockSpec(memory_space=pltpu.HBM)] * (sections + 2),
-        out_specs=(pl.BlockSpec(memory_space=pltpu.HBM), pl.BlockSpec(memory_space=pltpu.VMEM)),
+        out_specs=(pl.BlockSpec(memory_space=pltpu.VMEM), pl.BlockSpec(memory_space=pltpu.VMEM)),
         scratch_shapes=[pltpu.VMEM((n, rows, count), jnp.bfloat16) for count in counts]
         + [pltpu.VMEM(tile.shape, jnp.bfloat16) for tile in tiles]
         + [
@@ -258,18 +287,17 @@
             pltpu.VMEM((sections, rows, lead + tap_count + tail), jnp.bfloat16),
             pltpu.VMEM((sections, templates, bases), jnp.bfloat16),
             pltpu.VMEM((templates, counts[0]), jnp.float32),
-            pltpu.VMEM((templates, counts[0]), jnp.bfloat16),
             pltpu.VMEM((n, 1, counts[0]), jnp.float32),
-            pltpu.SemaphoreType.DMA((3 * sections + 1,)),
-            pltpu.SemaphoreType.DMA((sections,)),
-            pltpu.SemaphoreType.DMA((sections,)),
-            pltpu.SemaphoreType.DMA((sections,)),
-            pltpu.SemaphoreType.DMA((sections, n // 2)),
-            pltpu.SemaphoreType.DMA((sections,)),
+            pltpu.SemaphoreType.DMA((2 * sections + 1,)),
+            pltpu.SemaphoreType.DMA((pieces,)),
+            pltpu.SemaphoreType.DMA((pieces,)),
+            pltpu.SemaphoreType.DMA((pieces,)),
+            pltpu.SemaphoreType.DMA((pieces, n // 2)),
+            pltpu.SemaphoreType.DMA((pieces,)),
             pltpu.SemaphoreType.DMA((2,)),
         ],
-        compiler_params=pltpu.CompilerParams(collective_id=0, has_side_effects=True, vmem_limit_bytes=63500000),
-    )(*tiles, basis_taps, recon_coeffs)
+        compiler_params=pltpu.CompilerParams(collective_id=0, has_side_effects=True, vmem_limit_bytes=40000000),
+    )(*[pltpu.with_memory_space_constraint(array, pltpu.HBM) for array in (*tiles, basis_taps, recon_coeffs)])
     return snr, peak.reshape(counts[0])
 
 

time: 33.2 us -> 29.7 us (0.89)
  local copies, waits for them, and re-layouts: 3.13 us -> 1.39 us
  Pallas kernels: 29.2 us -> 27.5 us
    unnamed x2, local copies, waits for them, and re-layouts: 3.13 us -> 1.39 us
    pallas_call x1, Pallas kernels: 29.2 us -> 27.5 us  [fused(): pl.pallas_call(functools.partial(kernel, n, counts), out_shape=(jax.Shape...]
where the time goes in v2:
time: 29.7 us; the launch traced here: 29.5 us
  Pallas kernels  27.5 us (93%)
  local copies, waits for them, and re-layouts  1.39 us (5%)
  between operations  0.64 us (2%)
    pallas_call x1, Pallas kernels, fused(): pl.pallas_call(functools.partial(kernel, n, counts), out_shape=(jax.Shape...  27.5 us
    unnamed x2, local copies, waits for them, and re-layouts  1.39 us

profile of v2, /device:TPU:0, one launch (start us, length us, event | category | flops | bytes accessed | tf_op | source)
XLA Modules:
  0.0 29.5 jit_solution(13098046330068918284)
XLA Ops:
  0.6 27.5 %shard_map.77 = (bf16[256,1024]{1,0:T(8,128)(2,1)S(1)}, f32[1,1024]{1,0:T(1,128)S(1)}) custom-call(bf16[72,128]{1,0:T(8,128)(2,1)} %bitcast.6, bf16[68,128]{1,0:T(8,128)(2,1)} %bitcast.7, bf16[66,128]{1,0:T(8,128)(2,1)} %bitcast.8, bf16[65,128]{1,0:T(8,128)(2,1)} %bitcast.9, bf16[4,32,8192]{2,1,0:T(8,128)(2,1)} %refs_4_.1, bf16[4,256,512]{2,1,0:T(8,128)(2,1)} %refs_5_.1), custom_call_target="tpu_custom_call" | custom-call | tf_op jit(solution)/shard_map/pallas_call | solution.py:274
  28.1 0.8 %copy.10 = bf16[256,1024]{1,0:T(8,128)(2,1)} copy(bf16[256,1024]{1,0:T(8,128)(2,1)S(1)} %get-tuple-element.8) | data formatting | bytes 1048576
  28.9 0.6 %copy.11 = f32[1024]{0:T(1024)} copy(f32[1024]{0:T(1024)S(1)} %bitcast.5) | data formatting | bytes 8192

commit v3 on v2

--- a/solution.py
+++ b/solution.py
@@ -9,8 +9,9 @@
 
 LANES = 128
 BLOCK = 256
-UNROLL = 9
-PARTS = 3
+UNROLL = 18
+CUTS = 1, 1
+DEPTH = 16
 
 
 def shifted_rows(rows_ref, filled, tiles):
@@ -23,7 +24,7 @@
     for bit in range(3):
         moved = pltpu.roll(rows, width - (1 << bit), 1)
         rows = jnp.where((index >> bit) & 1 == 1, moved, rows)
-    return rows
+    return jnp.concatenate([rows, pltpu.roll(rows, width - 8, 1)], axis=0).astype(jnp.bfloat16)
 
 
 def doubled(values):
@@ -42,9 +43,14 @@
     sections = len(counts)
     x_hbm = refs[:sections]
     taps_hbm, coef_hbm, snr_ref, peak_ref = refs[sections : sections + 4]
-    gathered = refs[sections + 4 : 2 * sections + 4]
-    x_refs = refs[2 * sections + 4 : 3 * sections + 4]
-    scratch = refs[3 * sections + 4 :]
+    blocks = groups_of(counts)
+    gathered = refs[sections + 4 : sections + 4 + len(blocks)]
+    x_refs = refs[sections + 4 + len(blocks) : 2 * sections + 4 + len(blocks)]
+    scratch = refs[2 * sections + 4 + len(blocks) :]
+    places = {}
+    for b, block in enumerate(blocks):
+        for s in block:
+            places[s] = b, sum(counts[block[0] : s])
     wide, shifted, taps_ref, coef_ref, total_ref, peaks = scratch[:6]
     local_sem, along_sem, across_sem, mate_sem, recv_sem, pair_sem, peak_sem = scratch[6:]
     rows, tap_count = taps_hbm.shape[1], taps_hbm.shape[2]
@@ -86,47 +92,53 @@
         after = taps_ref.shape[2] - lead - tap_count
         taps_ref[s, :, lead + tap_count :] = jnp.zeros((rows, after), jnp.bfloat16)
 
-    def convolve(s, serve):
-        width = min(BLOCK, counts[s])
-        groups = counts[s] // width
+    def prepare(s):
         filled = x_refs[s].shape[0]
         x_in[s].wait()
         wide[:filled, :] = x_refs[s][...].astype(jnp.float32)
-        shifted[...] = shifted_rows(wide, filled, shifted.shape[1] // LANES)
+        shifted[s] = shifted_rows(wide, filled, shifted.shape[2] // LANES)
         taps_in[s].wait()
-        steps = -(-(groups - 1 + tap_count // BLOCK) // UNROLL)
+
+    def product(s, step):
+        width = min(BLOCK, counts[s])
         window = (2 * UNROLL + 2) * LANES
-
-        def body(step, total):
-            start = pl.multiple_of(step * (UNROLL * BLOCK), BLOCK)
-            base = shifted[:, pl.ds(start, window)]
-            grown = [base] + [pltpu.roll(base, window - 8 * g, 1) for g in range(1, LANES // 8)]
-            frames = jnp.concatenate(grown, axis=0).astype(jnp.bfloat16)
-            weights = jnp.concatenate([frames[:, at : at + width] for at in range(0, UNROLL * BLOCK, LANES)], axis=0)
-            left = jnp.concatenate(
-                [
-                    taps_ref[s, :, pl.ds(pl.multiple_of(start + (lead - a * BLOCK), BLOCK), UNROLL * BLOCK)]
-                    for a in range(groups)
-                ],
-                axis=0,
-            )
-            return total + jnp.dot(left, weights, preferred_element_type=jnp.float32)
-
-        total = jnp.zeros((groups * rows, width), jnp.float32)
-        cuts = [steps * part // PARTS for part in range(PARTS + 1)]
-        for part in range(PARTS):
-            total = lax.fori_loop(cuts[part], cuts[part + 1], body, total)
-            if part < PARTS - 1:
-                serve((s, part))
-        out = total.astype(jnp.bfloat16)
-        for a in range(groups):
-            gathered[s][me, :, a * width : (a + 1) * width] = out[a * rows : (a + 1) * rows]
+        start = pl.multiple_of(step * (UNROLL * BLOCK), BLOCK)
+        base = shifted[s, :, pl.ds(start, window)]
+        grown = [base] + [pltpu.roll(base, window - DEPTH * g, 1) for g in range(1, LANES // DEPTH)]
+        frames = jnp.concatenate(grown, axis=0)
+        weights = jnp.concatenate([frames[:, at : at + width] for at in range(0, UNROLL * BLOCK, LANES)], axis=0)
+        left = jnp.concatenate(
+            [
+                taps_ref[s, :, pl.ds(pl.multiple_of(start + (lead - a * BLOCK), BLOCK), UNROLL * BLOCK)]
+                for a in range(counts[s] // width)
+            ],
+            axis=0,
+        )
+        return jnp.dot(left, weights, preferred_element_type=jnp.float32)
+
+    def convolve(group):
+        for s in group:
+            prepare(s)
+        widths = [min(BLOCK, counts[s]) for s in group]
+        groups = [counts[s] // width for s, width in zip(group, widths)]
+        steps = max(-(-(g - 1 + tap_count // BLOCK) // UNROLL) for g in groups)
+
+        def body(step, totals):
+            return tuple(total + product(s, step) for s, total in zip(group, totals))
+
+        zeros = tuple(jnp.zeros((g * rows, width), jnp.float32) for g, width in zip(groups, widths))
+        totals = lax.fori_loop(0, steps, body, zeros)
+        for s, g, width, total in zip(group, groups, widths, totals):
+            out = total.astype(jnp.bfloat16)
+            b, at = places[s]
+            for a in range(g):
+                gathered[b][me, :, at + a * width : at + (a + 1) * width] = out[a * rows : (a + 1) * rows]
 
     chunks = chunks_of(counts, rows)
 
     def remote(c, slot, send_sem, recv_sem, to):
-        s, first, height = chunks[c]
-        part = gathered[s].at[slot, pl.ds(first, height)]
+        b, first, height = chunks[c]
+        part = gathered[b].at[slot, pl.ds(first, height)]
         return pltpu.make_async_remote_copy(
             src_ref=part,
             dst_ref=part,
@@ -187,41 +199,36 @@
                 pl.when(spot == at)(lambda count=count: remote(c, some(count), along_sem, pair_sem.at[c], mate).wait_send())
 
     def combine(s):
-        basis = gathered[s][...].reshape(n * rows, counts[s])
+        b, at = places[s]
+        basis = gathered[b][:, :, at : at + counts[s]].reshape(n * rows, counts[s])
         return jnp.dot(coef_ref[s], basis, preferred_element_type=jnp.float32)
 
     pieces = range(len(chunks))
-    early = {}
     order = []
     for k in range(1, lines):
         order += [(along, c, k) for c in pieces] + [(beside, c, k - 1) for c in pieces]
     order += [(beside, c, lines - 1) for c in pieces]
-    done = set()
-
-    def serve(at):
-        for event in early.get(at, []):
-            event[0](*event[1:])
-            done.add(event)
 
     running = {}
-    for s in range(sections):
-        convolve(s, serve)
-        if s == 0:
+    for b, block in enumerate(blocks):
+        convolve(block)
+        if b == 0:
             pl.semaphore_wait(barrier, greeted)
-        for c, chunk in enumerate(chunks):
-            if chunk[0] == s:
+        for c in pieces:
+            if chunks[c][0] == b:
                 own(c)
-        serve((s, PARTS - 1))
     coef_in.wait()
-    for event in order:
-        if event not in done:
-            event[0](*event[1:])
-    for c, chunk in enumerate(chunks):
-        to_mate(c, some(2 * lines)).wait_recv()
-        if chunk[0] == 0 and chunk[1] > 0 or chunk[2] == rows and chunk[0] == 0:
-            total_ref[...] = combine(0)
-        elif chunk[0] > 0:
-            running[chunk[0]] = combine(chunk[0])
+    for step, c, k in order:
+        step(c, k)
+    for b, block in enumerate(blocks):
+        for c in pieces:
+            if chunks[c][0] == b:
+                to_mate(c, some(2 * lines)).wait_recv()
+        for s in block:
+            if s == 0:
+                total_ref[...] = combine(0)
+            else:
+                running[s] = combine(s)
 
     upper = running[sections - 1]
     for s in reversed(range(1, sections - 1)):
@@ -250,10 +257,16 @@
     peak_ref[...] = jnp.max(peaks[...], axis=0)
 
 
+def groups_of(counts):
+    return (range(1), range(1, len(counts)))
+
+
 def chunks_of(counts, rows):
-    halves = 2 if rows % 32 == 0 else 1
-    height = rows // halves
-    return [(0, height * half, height) for half in range(halves)] + [(s, 0, rows) for s in range(1, len(counts))]
+    chunks = []
+    for b in range(len(groups_of(counts))):
+        cuts = CUTS[b] if rows % 32 == 0 else 1
+        chunks += [(b, rows // cuts * cut, rows // cuts) for cut in range(cuts)]
+    return chunks
 
 
 def tail_of(counts, tap_count):
@@ -279,11 +292,11 @@
         ),
         in_specs=[pl.BlockSpec(memory_space=pltpu.HBM)] * (sections + 2),
         out_specs=(pl.BlockSpec(memory_space=pltpu.VMEM), pl.BlockSpec(memory_space=pltpu.VMEM)),
-        scratch_shapes=[pltpu.VMEM((n, rows, count), jnp.bfloat16) for count in counts]
+        scratch_shapes=[pltpu.VMEM((n, rows, sum(counts[s] for s in block)), jnp.bfloat16) for block in groups_of(counts)]
         + [pltpu.VMEM(tile.shape, jnp.bfloat16) for tile in tiles]
         + [
             pltpu.VMEM((max(tile.shape[0] for tile in tiles), LANES), jnp.float32),
-            pltpu.VMEM((8, width), jnp.float32),
+            pltpu.VMEM((sections, DEPTH, width), jnp.bfloat16),
             pltpu.VMEM((sections, rows, lead + tap_count + tail), jnp.bfloat16),
             pltpu.VMEM((sections, templates, bases), jnp.bfloat16),
             pltpu.VMEM((templates, counts[0]), jnp.float32),

time: 29.7 us -> 28.6 us (0.963)
  Pallas kernels: 27.5 us -> 26.4 us
    pallas_call x1, Pallas kernels: 27.5 us -> 26.4 us  [fused(): pl.pallas_call(functools.partial(kernel, n, counts), out_shape=(jax.Shape...]
where the time goes in v3:
time: 28.6 us; the launch traced here: 28.4 us
  Pallas kernels  26.4 us (92%)
  local copies, waits for them, and re-layouts  1.39 us (5%)
  between operations  0.64 us (2%)
    pallas_call x1, Pallas kernels, fused(): pl.pallas_call(functools.partial(kernel, n, counts), out_shape=(jax.Shape...  26.4 us
    unnamed x2, local copies, waits for them, and re-layouts  1.39 us

profile of v3, /device:TPU:0, one launch (start us, length us, event | category | flops | bytes accessed | tf_op | source)
XLA Modules:
  0.0 28.4 jit_solution(5500731555326309064)
XLA Ops:
  0.6 26.4 %shard_map.77 = (bf16[256,1024]{1,0:T(8,128)(2,1)S(1)}, f32[1,1024]{1,0:T(1,128)S(1)}) custom-call(bf16[72,128]{1,0:T(8,128)(2,1)} %bitcast.6, bf16[68,128]{1,0:T(8,128)(2,1)} %bitcast.7, bf16[66,128]{1,0:T(8,128)(2,1)} %bitcast.8, bf16[65,128]{1,0:T(8,128)(2,1)} %bitcast.9, bf16[4,32,8192]{2,1,0:T(8,128)(2,1)} %refs_4_.1, bf16[4,256,512]{2,1,0:T(8,128)(2,1)} %refs_5_.1), custom_call_target="tpu_custom_call" | custom-call | tf_op jit(solution)/shard_map/pallas_call | solution.py:287
  27.0 0.8 %copy.10 = bf16[256,1024]{1,0:T(8,128)(2,1)} copy(bf16[256,1024]{1,0:T(8,128)(2,1)S(1)} %get-tuple-element.8) | data formatting | bytes 1048576
  27.8 0.6 %copy.11 = f32[1024]{0:T(1024)} copy(f32[1024]{0:T(1024)S(1)} %bitcast.5) | data formatting | bytes 8192
